TPU v7x, 512 devices: a whole 4x4x16 slice. The times are simulated.
512 devices in a mesh: dp: 4 (over x), mp: 128 (over z, y, core).
Axes of the slice: x: 4, y: 4, z: 16, core: 2. Of those that a mesh axis runs over, the one named last changes fastest.
Arguments:
- acts: bfloat16 [8192, 16384], P('dp', 'mp'), may hold values from -6 to 6
- diag_weight: bfloat16 [7, 16384, 128], P(None, 'mp'), may hold values from -0.375 to 0.375
- cross_weight: bfloat16 [7, 16384, 128], P(None, 'mp'), may hold values from -0.375 to 0.375
- low_in: bfloat16 [16384, 64], P('mp'), may hold values from -0.046875 to 0.046875
- low_out: bfloat16 [64, 16384], P(None, 'mp'), may hold values from -0.75 to 0.75
- cotangent: bfloat16 [8192, 16384], P('dp', 'mp'), may hold values from -6 to 6
Outputs:
- output: bfloat16 [8192, 16384], P('dp', 'mp')
- grad_acts: bfloat16 [8192, 16384], P('dp', 'mp')
- grad_diag: float32 [7, 16384, 128], P(None, 'mp')
- grad_cross: float32 [7, 16384, 128], P(None, 'mp')
- grad_low_in: float32 [16384, 64], P('mp')
- grad_low_out: float32 [64, 16384], P(None, 'mp')
All inputs are finite; a program needn't handle non-finite values.
Results may differ from a plain program's by a relative error of at most 0.019.
Values may be sent and summed in bfloat16 or wider, within the bound.
A program may use at most 64 MiB of HBM per device.

v0:
```python
import jax
import jax.numpy as jnp
from jax import lax
from jax.sharding import PartitionSpec as P


def swapped(block, axis, stride):
    count = lax.axis_size(axis)
    route = []
    for low in range(count):
        high = low | 1 << stride
        if high != low and high < count:
            route += [(low, high), (high, low)]
    return lax.ppermute(block, axis, route)


def gelu_slope(pre, cot):
    return jax.vjp(lambda v: jax.nn.gelu(v, approximate=True), pre)[1](cot)[0]


def summed(partial):
    piece = lax.psum_scatter(partial, "mp", scatter_dimension=0, tiled=True)
    return lax.all_gather(piece.astype(jnp.bfloat16), "mp", axis=0, tiled=True)


def rank_total(acts, low_in):
    partial_low = jnp.dot(acts, low_in, preferred_element_type=jnp.float32)
    return summed(partial_low)


def per_device(acts, diag_weight, cross_weight, low_in, low_out, cotangent):
    sections = lax.axis_size("mp").bit_length() - 1
    scale = float(acts.shape[0] * lax.axis_size("dp")) ** (-0.5)
    low = None
    state = acts
    saved = []
    partners = []
    mixed = None
    for section in range(sections):
        other = swapped(state, "mp", section)
        saved.append(state)
        partners.append(other)
        fresh = jnp.dot(state, diag_weight[section], preferred_element_type=jnp.float32)
        fresh = fresh + jnp.dot(other, cross_weight[section], preferred_element_type=jnp.float32)
        if section < sections - 1:
            state = fresh.astype(jnp.bfloat16)
        else:
            mixed = fresh
    low = rank_total(acts, low_in)
    low_b = low.astype(jnp.bfloat16)
    pre = mixed + jnp.dot(low_b, low_out, preferred_element_type=jnp.float32)
    output = jax.nn.gelu(pre, approximate=True).astype(jnp.bfloat16)
    d_pre = gelu_slope(pre, cotangent.astype(jnp.float32)).astype(jnp.bfloat16)
    partial_back = jnp.dot(d_pre, low_out.T, preferred_element_type=jnp.float32)
    d_low = summed(partial_back)
    low_back = jnp.dot(d_low, low_in.T, preferred_element_type=jnp.float32)
    local_in = scale * jnp.dot(acts.T, d_low, preferred_element_type=jnp.float32)
    local_out = scale * jnp.dot(low_b.T, d_pre, preferred_element_type=jnp.float32)
    grad_low_in, grad_low_out = (
        lax.psum(local_in.astype(jnp.bfloat16), "dp").astype(jnp.float32),
        lax.psum(local_out.astype(jnp.bfloat16), "dp").astype(jnp.float32),
    )
    upper = d_pre
    grads_d = [None] * sections
    grads_c = [None] * sections
    grad_acts = None
    for section in range(sections - 1, -1, -1):
        term_d = scale * jnp.dot(saved[section].T, upper, preferred_element_type=jnp.float32)
        term_c = scale * jnp.dot(partners[section].T, upper, preferred_element_type=jnp.float32)
        term_d, term_c = (
            lax.psum(term_d.astype(jnp.bfloat16), "dp").astype(jnp.float32),
            lax.psum(term_c.astype(jnp.bfloat16), "dp").astype(jnp.float32),
        )
        grads_d[section] = term_d
        grads_c[section] = term_c
        sent = jnp.dot(upper, cross_weight[section].T, preferred_element_type=jnp.float32).astype(
            jnp.bfloat16
        )
        arrived = swapped(sent, "mp", section)
        back = jnp.dot(
            upper, diag_weight[section].T, preferred_element_type=jnp.float32
        ) + arrived.astype(jnp.float32)
        if section > 0:
            upper = back.astype(jnp.bfloat16)
        else:
            grad_acts = (back + low_back).astype(jnp.bfloat16)
    grad_diag = jnp.stack(grads_d)
    grad_cross = jnp.stack(grads_c)
    return (output, grad_acts, grad_diag, grad_cross, grad_low_in, grad_low_out)


def solution(mesh):
    placed = (
        P("dp", "mp"),
        P(None, "mp", None),
        P(None, "mp", None),
        P("mp", None),
        P(None, "mp"),
        P("dp", "mp"),
    )
    return jax.shard_map(
        per_device,
        mesh=mesh,
        in_specs=placed,
        out_specs=(
            P("dp", "mp"),
            P("dp", "mp"),
            P(None, "mp", None),
            P(None, "mp", None),
            P("mp", None),
            P(None, "mp"),
        ),
        check_vma=False,
    )
```

profile of v0, /device:TPU:8, one launch (start us, length us, event | category | flops | bytes accessed | tf_op | source)
XLA Modules:
  0.0 965.8 jit_solution(15311273889378741607)
XLA Ops:
  7.2 2.1 collective-permute-start
  12.2 7.7 collective-permute-start.1
  20.2 11.9 %collective-permute-done.1 = bf16[2048,128]{1,0:T(8,128)(2,1)S(1)} collective-permute-done((bf16[2048,128]{1,0:T(8,128)(2,1)S(1)}, bf16[2048,128]{1,0:T(8,128)(2,1)S(1)}, u32[]{:S(2)}, u32[]{:S(2)}) %collective-permute-start.1) | collective-permute-done | bytes 524320 | tf_op jit(solution)/shard_map/ppermute | solution.py:14
  35.1 14.7 %collective-permute-done.2 = bf16[2048,128]{1,0:T(8,128)(2,1)S(1)} collective-permute-done((bf16[2048,128]{1,0:T(8,128)(2,1)S(1)}, bf16[2048,128]{1,0:T(8,128)(2,1)S(1)}, u32[]{:S(2)}, u32[]{:S(2)}) %collective-permute-start.2) | collective-permute-done | bytes 524320 | tf_op jit(solution)/shard_map/ppermute | solution.py:14
  52.8 12.2 %collective-permute-done.3 = bf16[2048,128]{1,0:T(8,128)(2,1)S(1)} collective-permute-done((bf16[2048,128]{1,0:T(8,128)(2,1)S(1)}, bf16[2048,128]{1,0:T(8,128)(2,1)S(1)}, u32[]{:S(2)}, u32[]{:S(2)}) %collective-permute-start.3) | collective-permute-done | bytes 524320 | tf_op jit(solution)/shard_map/ppermute | solution.py:14
  68.0 23.4 %collective-permute-done.4 = bf16[2048,128]{1,0:T(8,128)(2,1)S(1)} collective-permute-done((bf16[2048,128]{1,0:T(8,128)(2,1)S(1)}, bf16[2048,128]{1,0:T(8,128)(2,1)S(1)}, u32[]{:S(2)}, u32[]{:S(2)}) %collective-permute-start.4) | collective-permute-done | bytes 524320 | tf_op jit(solution)/shard_map/ppermute | solution.py:14
  92.2 5.0 collective-permute-start.5
  98.9 44.4 %collective-permute-done.5 = bf16[2048,128]{1,0:T(8,128)(2,1)} collective-permute-done((bf16[2048,128]{1,0:T(8,128)(2,1)S(1)}, bf16[2048,128]{1,0:T(8,128)(2,1)}, u32[]{:S(2)}, u32[]{:S(2)}) %collective-permute-start.5) | collective-permute-done | bytes 524320 | tf_op jit(solution)/shard_map/ppermute | solution.py:14
  144.6 22.4 %collective-permute-start.6 = (bf16[2048,128]{1,0:T(8,128)(2,1)S(1)}, bf16[2048,128]{1,0:T(8,128)(2,1)}, u32[]{:S(2)}, u32[]{:S(2)}) collective-permute-start(bf16[2048,128]{1,0:T(8,128)(2,1)S(1)} %fusion.6), channel_id=1, source_target_pairs={{0,64},{64,0},{1,65},{65,1},{2,66},{66,2},{3,67},{67,3},{4,68},{68... | collective-permute-start | bytes 1572872 | tf_op jit(solution)/shard_map/ppermute | solution.py:14
  167.1 190.0 %reduce-scatter.3.cloned.1.call-done = f32[16,64]{1,0:T(8,128)} async-done(((f32[2048,64]{1,0:T(8,128)}), f32[16,64]{1,0:T(8,128)}) %reduce-scatter.3.cloned.1.call-update) | async-done | bytes 4112 | tf_op jit(solution)/shard_map/reduce_scatter | solution.py:22
  357.8 81.0 %all_gather.6 = bf16[2048,64]{1,0:T(8,128)(2,1)S(1)} all-gather(bf16[16,64]{1,0:T(8,128)(2,1)S(1)} %convert_element_type.179), channel_id=1, replica_groups=mesh['dp'=4,'mp'=128] {'mp'}, dimensions={0}, use_global_device_ids=true | all-gather | bytes 264192 | tf_op jit(solution)/shard_map/all_gather | solution.py:23
  442.6 10.4 %collective-permute-start.7 = (bf16[2048,128]{1,0:T(8,128)(2,1)S(1)}, bf16[2048,128]{1,0:T(8,128)(2,1)S(1)}, u32[]{:S(2)}, u32[]{:S(2)}) collective-permute-start(bf16[2048,128]{1,0:T(8,128)(2,1)S(1)} %convolution_convert_fusion.6), channel_id=1, source_target_pairs={{0,64},{64,0},{1,65},{65,1},{2,66},{66,2},{3,67},{67,3},{4,68},{68... | collective-permute-start | bytes 1572872 | tf_op jit(solution)/shard_map/ppermute | solution.py:14
  453.1 44.2 %collective-permute-done.7 = bf16[2048,128]{1,0:T(8,128)(2,1)S(1)} collective-permute-done((bf16[2048,128]{1,0:T(8,128)(2,1)S(1)}, bf16[2048,128]{1,0:T(8,128)(2,1)S(1)}, u32[]{:S(2)}, u32[]{:S(2)}) %collective-permute-start.7) | collective-permute-done | bytes 524320 | tf_op jit(solution)/shard_map/ppermute | solution.py:14
  497.9 4.7 collective-permute-start.8
  503.9 43.8 %collective-permute-done.8 = bf16[2048,128]{1,0:T(8,128)(2,1)} collective-permute-done((bf16[2048,128]{1,0:T(8,128)(2,1)S(1)}, bf16[2048,128]{1,0:T(8,128)(2,1)}, u32[]{:S(2)}, u32[]{:S(2)}) %collective-permute-start.8) | collective-permute-done | bytes 524320 | tf_op jit(solution)/shard_map/ppermute | solution.py:14
  552.3 2.0 fusion.27
  555.3 18.4 %collective-permute-done.9 = bf16[2048,128]{1,0:T(8,128)(2,1)S(1)} collective-permute-done((bf16[2048,128]{1,0:T(8,128)(2,1)S(1)}, bf16[2048,128]{1,0:T(8,128)(2,1)S(1)}, u32[]{:S(2)}, u32[]{:S(2)}) %collective-permute-start.9) | collective-permute-done | bytes 524320 | tf_op jit(solution)/shard_map/ppermute | solution.py:14
  580.7 183.4 %reduce-scatter.5.cloned.1.call-done = f32[16,64]{1,0:T(8,128)} async-done(((f32[2048,64]{1,0:T(8,128)}), f32[16,64]{1,0:T(8,128)}) %reduce-scatter.5.cloned.1.call-update) | async-done | bytes 4112 | tf_op jit(solution)/shard_map/reduce_scatter | solution.py:22
  764.8 81.2 %all_gather.7 = bf16[2048,64]{1,0:T(8,128)(2,1)S(1)} all-gather(bf16[16,64]{1,0:T(8,128)(2,1)S(1)} %convert_element_type.203), channel_id=1, replica_groups=mesh['dp'=4,'mp'=128] {'mp'}, dimensions={0}, use_global_device_ids=true | all-gather | bytes 264192 | tf_op jit(solution)/shard_map/all_gather | solution.py:23
  848.6 4.1 collective-permute-start.11
  856.8 9.5 collective-permute-done.11
  867.7 3.9 collective-permute-start.12
  875.5 7.7 collective-permute-done.12
  888.8 55.6 %all-reduce.3.cloned.1.call-done = (bf16[1,128,128]{1,2,0:T(8,128)(2,1)}, bf16[1,128,128]{1,2,0:T(8,128)(2,1)}, bf16[1,128,128]{1,2,0:T(8,128)(2,1)}, bf16[1,128...) async-done(((bf16[1,128,128]{1,2,0:T(8,128)(2,1)}, ...) | async-done | bytes 491536 | tf_op jit(solution)/shard_map/psum | solution.py:71
  (164 shorter events, 67.8 us)
Async XLA Ops:
  7.2 433.3 %copy-start = (bf16[64,128]{1,0:T(8,128)(2,1)S(1)}, bf16[64,128]{1,0:T(8,128)(2,1)}, u32[]{:S(2)}) copy-start(bf16[64,128]{1,0:T(8,128)(2,1)} %param.10) | copy-start | bytes 49156
  7.2 349.9 %reduce-scatter.3.cloned.1.call-start = ((), (), s32[]{:S(2)}) async-start(), calls=%async_computation.2 | async-start | bytes 1056768 | tf_op jit(solution)/shard_map/reduce_scatter | solution.py:22
  7.2 4.1 collective-permute-start
  10.6 9.3 copy-start.23
  12.2 19.9 %collective-permute-start.1 = (bf16[2048,128]{1,0:T(8,128)(2,1)S(1)}, bf16[2048,128]{1,0:T(8,128)(2,1)S(1)}, u32[]{:S(2)}, u32[]{:S(2)}) collective-permute-start(bf16[2048,128]{1,0:T(8,128)(2,1)S(1)} %fusion.1), channel_id=1, source_target_pairs={{0,2},{2,0},{1,3},{3,1},{4,6},{6,4},{5,7},{7,5},{8,10},{10,8},{9,1... | collective-permute-start | bytes 1572872 | tf_op jit(solution)/shard_map/ppermute | solution.py:14
  32.9 16.8 %collective-permute-start.2 = (bf16[2048,128]{1,0:T(8,128)(2,1)S(1)}, bf16[2048,128]{1,0:T(8,128)(2,1)S(1)}, u32[]{:S(2)}, u32[]{:S(2)}) collective-permute-start(bf16[2048,128]{1,0:T(8,128)(2,1)S(1)} %fusion.2), channel_id=1, source_target_pairs={{0,4},{4,0},{1,5},{5,1},{2,6},{6,2},{3,7},{7,3},{8,12},{12,8},{9,1... | collective-permute-start | bytes 1572872 | tf_op jit(solution)/shard_map/ppermute | solution.py:14
  50.6 14.4 %collective-permute-start.3 = (bf16[2048,128]{1,0:T(8,128)(2,1)S(1)}, bf16[2048,128]{1,0:T(8,128)(2,1)S(1)}, u32[]{:S(2)}, u32[]{:S(2)}) collective-permute-start(bf16[2048,128]{1,0:T(8,128)(2,1)S(1)} %fusion.3), channel_id=1, source_target_pairs={{0,8},{8,0},{1,9},{9,1},{2,10},{10,2},{3,11},{11,3},{4,12},{12,4},... | collective-permute-start | bytes 1572872 | tf_op jit(solution)/shard_map/ppermute | solution.py:14
  65.8 25.6 %collective-permute-start.4 = (bf16[2048,128]{1,0:T(8,128)(2,1)S(1)}, bf16[2048,128]{1,0:T(8,128)(2,1)S(1)}, u32[]{:S(2)}, u32[]{:S(2)}) collective-permute-start(bf16[2048,128]{1,0:T(8,128)(2,1)S(1)} %fusion.4), channel_id=1, source_target_pairs={{0,16},{16,0},{1,17},{17,1},{2,18},{18,2},{3,19},{19,3},{4,20},{20... | collective-permute-start | bytes 1572872 | tf_op jit(solution)/shard_map/ppermute | solution.py:14
  68.0 29.3 %copy-start.1 = (bf16[2048,128]{1,0:T(8,128)(2,1)S(1)}, bf16[2048,128]{1,0:T(8,128)(2,1)}, u32[]{:S(2)}) copy-start(bf16[2048,128]{1,0:T(8,128)(2,1)} %param.6) | copy-start | bytes 1572868
  68.0 29.3 %copy-start.24 = (bf16[128,64]{0,1:T(8,128)(2,1)S(1)}, bf16[128,64]{0,1:T(8,128)(2,1)}, u32[]{:S(2)}) copy-start(bf16[128,64]{0,1:T(8,128)(2,1)} %param.9) | copy-start | bytes 49156
  92.2 6.4 copy-start.6
  92.2 51.1 %collective-permute-start.5 = (bf16[2048,128]{1,0:T(8,128)(2,1)S(1)}, bf16[2048,128]{1,0:T(8,128)(2,1)}, u32[]{:S(2)}, u32[]{:S(2)}) collective-permute-start(bf16[2048,128]{1,0:T(8,128)(2,1)S(1)} %fusion.5), channel_id=1, source_target_pairs={{0,32},{32,0},{1,33},{33,1},{2,34},{34,2},{3,35},{35,3},{4,36},{36... | collective-permute-start | bytes 1572872 | tf_op jit(solution)/shard_map/ppermute | solution.py:14
  98.6 665.5 %reduce-scatter.5.cloned.1.call-start = ((), (), s32[]{:S(2)}) async-start(), calls=%async_computation.3 | async-start | bytes 1056768 | tf_op jit(solution)/shard_map/reduce_scatter | solution.py:22
  144.6 294.4 %copy-start.8 = (bf16[2048,128]{1,0:T(8,128)(2,1)}, bf16[2048,128]{1,0:T(8,128)(2,1)S(1)}, u32[]{:S(2)}) copy-start(bf16[2048,128]{1,0:T(8,128)(2,1)S(1)} %fusion.6) | copy-start | bytes 1572868
  144.6 294.4 %collective-permute-start.6 = (bf16[2048,128]{1,0:T(8,128)(2,1)S(1)}, bf16[2048,128]{1,0:T(8,128)(2,1)}, u32[]{:S(2)}, u32[]{:S(2)}) collective-permute-start(bf16[2048,128]{1,0:T(8,128)(2,1)S(1)} %fusion.6), channel_id=1, source_target_pairs={{0,64},{64,0},{1,65},{65,1},{2,66},{66,2},{3,67},{67,3},{4,68},{68... | collective-permute-start | bytes 1572872 | tf_op jit(solution)/shard_map/ppermute | solution.py:14
  442.6 54.6 %collective-permute-start.7 = (bf16[2048,128]{1,0:T(8,128)(2,1)S(1)}, bf16[2048,128]{1,0:T(8,128)(2,1)S(1)}, u32[]{:S(2)}, u32[]{:S(2)}) collective-permute-start(bf16[2048,128]{1,0:T(8,128)(2,1)S(1)} %convolution_convert_fusion.6), channel_id=1, source_target_pairs={{0,64},{64,0},{1,65},{65,1},{2,66},{66,2},{3,67},{67,3},{4,68},{68... | collective-permute-start | bytes 1572872 | tf_op jit(solution)/shard_map/ppermute | solution.py:14
  497.9 49.9 %collective-permute-start.8 = (bf16[2048,128]{1,0:T(8,128)(2,1)S(1)}, bf16[2048,128]{1,0:T(8,128)(2,1)}, u32[]{:S(2)}, u32[]{:S(2)}) collective-permute-start(bf16[2048,128]{1,0:T(8,128)(2,1)S(1)} %convolution_convert_fusion.5), channel_id=1, source_target_pairs={{0,32},{32,0},{1,33},{33,1},{2,34},{34,2},{3,35},{35,3},{4,36},{36... | collective-permute-start | bytes 1572872 | tf_op jit(solution)/shard_map/ppermute | solution.py:14
  503.9 440.4 %all-reduce.3.cloned.1.call-start = ((), (), s32[]{:S(2)}) async-start(), calls=%async_computation.4 | async-start | bytes 983040 | tf_op jit(solution)/shard_map/psum | solution.py:71
  549.4 24.2 %collective-permute-start.9 = (bf16[2048,128]{1,0:T(8,128)(2,1)S(1)}, bf16[2048,128]{1,0:T(8,128)(2,1)S(1)}, u32[]{:S(2)}, u32[]{:S(2)}) collective-permute-start(bf16[2048,128]{1,0:T(8,128)(2,1)S(1)} %convolution_convert_fusion.4), channel_id=1, source_target_pairs={{0,16},{16,0},{1,17},{17,1},{2,18},{18,2},{3,19},{19,3},{4,20},{20... | collective-permute-start | bytes 1572872 | tf_op jit(solution)/shard_map/ppermute | solution.py:14
  575.8 271.1 %collective-permute-start.10 = (bf16[2048,128]{1,0:T(8,128)(2,1)}, bf16[2048,128]{1,0:T(8,128)(2,1)}, u32[]{:S(2)}, u32[]{:S(2)}) collective-permute-start(bf16[2048,128]{1,0:T(8,128)(2,1)} %convolution_convert_fusion.3), channel_id=1, source_target_pairs={{0,8},{8,0},{1,9},{9,1},{2,10},{10,2},{3,11},{11,3},{4,12},{12,4},... | collective-permute-start | bytes 1572872 | tf_op jit(solution)/shard_map/ppermute | solution.py:14
  848.6 5.1 copy-start.21
  848.6 17.7 %collective-permute-start.11 = (bf16[2048,128]{1,0:T(8,128)(2,1)S(1)}, bf16[2048,128]{1,0:T(8,128)(2,1)S(1)}, u32[]{:S(2)}, u32[]{:S(2)}) collective-permute-start(bf16[2048,128]{1,0:T(8,128)(2,1)S(1)} %convolution_convert_fusion.2), channel_id=1, source_target_pairs={{0,4},{4,0},{1,5},{5,1},{2,6},{6,2},{3,7},{7,3},{8,12},{12,8},{9,1... | collective-permute-start | bytes 1572872 | tf_op jit(solution)/shard_map/ppermute | solution.py:14
  867.7 15.5 %collective-permute-start.12 = (bf16[2048,128]{1,0:T(8,128)(2,1)S(1)}, bf16[2048,128]{1,0:T(8,128)(2,1)S(1)}, u32[]{:S(2)}, u32[]{:S(2)}) collective-permute-start(bf16[2048,128]{1,0:T(8,128)(2,1)S(1)} %convolution_convert_fusion.1), channel_id=1, source_target_pairs={{0,2},{2,0},{1,3},{3,1},{4,6},{6,4},{5,7},{7,5},{8,10},{10,8},{9,1... | collective-permute-start | bytes 1572872 | tf_op jit(solution)/shard_map/ppermute | solution.py:14
  886.8 70.6 %collective-permute-start.13 = (bf16[2048,128]{1,0:T(8,128)(2,1)S(1)}, bf16[2048,128]{1,0:T(8,128)(2,1)S(1)}, u32[]{:S(2)}, u32[]{:S(2)}) collective-permute-start(bf16[2048,128]{1,0:T(8,128)(2,1)S(1)} %convolution_convert_fusion), channel_id=1, source_target_pairs={{0,1},{1,0},{2,3},{3,2},{4,5},{5,4},{6,7},{7,6},{8,9},{9,8},{10,11... | collective-permute-start | bytes 1572872 | tf_op jit(solution)/shard_map/ppermute | solution.py:14
  (34 other events, 48.5 us)
Sparse Core Ops, SparseCore 0:
  98.7 258.3 reduce-scatter.2
  504.0 260.0 reduce-scatter.4
  886.4 57.8 all-reduce.2
where the time goes:
time: 968 us; the launch traced here: 966 us
  waiting for transfers between devices  660 us (68%)
  blocking collectives  162 us (17%)
  starting transfers between devices  72 us (7%)
  matrix products  40.1 us (4%)
  between operations  14.3 us (1%)
  local copies, waits for them, and re-layouts  14 us (1%)
    reduce_scatter x2, waiting for transfers between devices, summed(): piece = lax.psum_scatter(partial, 'mp', scatter_dimension=0, tiled=True)  373 us
    ppermute x14, waiting for transfers between devices, swapped(): return lax.ppermute(block, axis, route)  231 us
    all_gather x2, blocking collectives, summed(): return lax.all_gather(piece.astype(jnp.bfloat16), 'mp', axis=0, tiled=True)  162 us
    ppermute x14, starting transfers between devices, swapped(): return lax.ppermute(block, axis, route)  71.9 us
    psum x1, waiting for transfers between devices, per_device(): lax.psum(term_d.astype(jnp.bfloat16), 'dp').astype(jnp.float32)  55.6 us
  transfers between devices with their start and end apart: 17, of which 14 were waited for; matrix products, arithmetic and copies ran while one was open for 3% of the time, Pallas kernels for 0%

commit v1 on v0

--- a/solution.py
+++ b/solution.py
@@ -2,6 +2,13 @@
 import jax.numpy as jnp
 from jax import lax
 from jax.sharding import PartitionSpec as P
+
+
+def exchange_gather(shard, mesh_axis, along):
+    n_dev = lax.axis_size(mesh_axis)
+    tiles = jnp.stack([shard for _ in range(n_dev)])
+    tiles = lax.all_to_all(tiles, mesh_axis, split_axis=0, concat_axis=0)
+    return jnp.concatenate(tiles, axis=along)
 
 
 def swapped(block, axis, stride):
@@ -20,7 +27,7 @@
 
 def summed(partial):
     piece = lax.psum_scatter(partial, "mp", scatter_dimension=0, tiled=True)
-    return lax.all_gather(piece.astype(jnp.bfloat16), "mp", axis=0, tiled=True)
+    return exchange_gather(piece.astype(jnp.bfloat16), "mp", 0)
 
 
 def rank_total(acts, low_in):

time: 968 us -> 869 us (0.90)
  blocking collectives: 162 us -> 0 us
  waiting for transfers between devices: 660 us -> 705 us
    all_gather x2 -> x0, blocking collectives: 162 us -> none  [summed(): return lax.all_gather(piece.astype(jnp.bfloat16), 'mp', axis=0, tiled=True)]
    reduce_scatter x2, waiting for transfers between devices: 373 us -> 418 us  [summed(): piece = lax.psum_scatter(partial, 'mp', scatter_dimension=0, tiled=True)]
    all_to_all x0 -> x2, starting transfers between devices: none -> 27.1 us  [exchange_gather(): tiles = lax.all_to_all(tiles, mesh_axis, split_axis=0, concat_axis=0)]
    ppermute x14, starting transfers between devices: 71.9 us -> 54 us  [swapped(): return lax.ppermute(block, axis, route)]
    ppermute x14, waiting for transfers between devices: 231 us -> 214 us  [swapped(): return lax.ppermute(block, axis, route)]
    all_to_all x0 -> x2, waiting for transfers between devices: none -> 16.4 us  [exchange_gather(): tiles = lax.all_to_all(tiles, mesh_axis, split_axis=0, concat_axis=0)]
  transfers between devices with their start and end apart: 17 -> 19, of which waited for: 14 -> 16; matrix products, arithmetic and copies ran while one was open for 3% -> 5% of each run, Pallas kernels for 0% -> 0%
where the time goes in v1:
time: 869 us; the launch traced here: 866 us
  waiting for transfers between devices  705 us (81%)
  starting transfers between devices  81.2 us (9%)
  matrix products  42.5 us (5%)
  local copies, waits for them, and re-layouts  20.1 us (2%)
  between operations  14.3 us (2%)
    reduce_scatter x2, waiting for transfers between devices, summed(): piece = lax.psum_scatter(partial, 'mp', scatter_dimension=0, tiled=True)  418 us
    ppermute x14, waiting for transfers between devices, swapped(): return lax.ppermute(block, axis, route)  214 us
    psum x1, waiting for transfers between devices, per_device(): lax.psum(term_d.astype(jnp.bfloat16), 'dp').astype(jnp.float32)  56 us
    ppermute x14, starting transfers between devices, swapped(): return lax.ppermute(block, axis, route)  54 us
    all_to_all x2, starting transfers between devices, exchange_gather(): tiles = lax.all_to_all(tiles, mesh_axis, split_axis=0, concat_axis=0)  27.1 us
    unnamed x110, local copies, waits for them, and re-layouts  19.1 us
  transfers between devices with their start and end apart: 19, of which 16 were waited for; matrix products, arithmetic and copies ran while one was open for 5% of the time, Pallas kernels for 0%

profile of v1, /device:TPU:8, one launch (start us, length us, event | category | flops | bytes accessed | tf_op | source)
XLA Modules:
  0.0 866.3 jit_solution(6359849745290136738)
XLA Ops:
  7.2 2.1 collective-permute-start
  12.2 7.7 collective-permute-start.1
  20.2 11.9 %collective-permute-done.1 = bf16[2048,128]{1,0:T(8,128)(2,1)S(1)} collective-permute-done((bf16[2048,128]{1,0:T(8,128)(2,1)S(1)}, bf16[2048,128]{1,0:T(8,128)(2,1)S(1)}, u32[]{:S(2)}, u32[]{:S(2)}) %collective-permute-start.1) | collective-permute-done | bytes 524320 | tf_op jit(solution)/shard_map/ppermute | solution.py:21
  35.1 14.7 %collective-permute-done.2 = bf16[2048,128]{1,0:T(8,128)(2,1)S(1)} collective-permute-done((bf16[2048,128]{1,0:T(8,128)(2,1)S(1)}, bf16[2048,128]{1,0:T(8,128)(2,1)S(1)}, u32[]{:S(2)}, u32[]{:S(2)}) %collective-permute-start.2) | collective-permute-done | bytes 524320 | tf_op jit(solution)/shard_map/ppermute | solution.py:21
  52.8 12.2 %collective-permute-done.3 = bf16[2048,128]{1,0:T(8,128)(2,1)S(1)} collective-permute-done((bf16[2048,128]{1,0:T(8,128)(2,1)S(1)}, bf16[2048,128]{1,0:T(8,128)(2,1)S(1)}, u32[]{:S(2)}, u32[]{:S(2)}) %collective-permute-start.3) | collective-permute-done | bytes 524320 | tf_op jit(solution)/shard_map/ppermute | solution.py:21
  69.4 22.1 %collective-permute-done.4 = bf16[2048,128]{1,0:T(8,128)(2,1)S(1)} collective-permute-done((bf16[2048,128]{1,0:T(8,128)(2,1)S(1)}, bf16[2048,128]{1,0:T(8,128)(2,1)S(1)}, u32[]{:S(2)}, u32[]{:S(2)}) %collective-permute-start.4) | collective-permute-done | bytes 524320 | tf_op jit(solution)/shard_map/ppermute | solution.py:21
  92.3 5.0 collective-permute-start.5
  97.3 232.8 %reduce-scatter.3.cloned.1.call-done = f32[16,64]{1,0:T(8,128)} async-done(((f32[2048,64]{1,0:T(8,128)}), f32[16,64]{1,0:T(8,128)}) %reduce-scatter.3.cloned.1.call-update) | async-done | bytes 4112 | tf_op jit(solution)/shard_map/reduce_scatter | solution.py:29
  331.8 13.5 %all-to-all-start = ((bf16[128,2,512]{2,1,0:T(2,128)(2,1)}), bf16[128,2,512]{2,1,0:T(2,128)(2,1)S(1)}, u32[]{:S(2)}, u32[]{:S(2)}) async-start(bf16[128,2,512]{2,1,0:T(2,128)(2,1)} %reshape.24), calls=%async_computation.1 | async-start | bytes 524288 | tf_op jit(solution)/shard_map/all_to_all | solution.py:10
  347.5 12.4 %collective-permute-start.6 = (bf16[2048,128]{1,0:T(8,128)(2,1)S(1)}, bf16[2048,128]{1,0:T(8,128)(2,1)S(1)}, u32[]{:S(2)}, u32[]{:S(2)}) collective-permute-start(bf16[2048,128]{1,0:T(8,128)(2,1)S(1)} %fusion.6), channel_id=1, source_target_pairs={{0,64},{64,0},{1,65},{65,1},{2,66},{66,2},{3,67},{67,3},{4,68},{68... | collective-permute-start | bytes 1572872 | tf_op jit(solution)/shard_map/ppermute | solution.py:21
  360.0 6.6 all-to-all-done
  368.8 43.5 %collective-permute-done.6 = bf16[2048,128]{1,0:T(8,128)(2,1)S(1)} collective-permute-done((bf16[2048,128]{1,0:T(8,128)(2,1)S(1)}, bf16[2048,128]{1,0:T(8,128)(2,1)S(1)}, u32[]{:S(2)}, u32[]{:S(2)}) %collective-permute-start.6) | collective-permute-done | bytes 524320 | tf_op jit(solution)/shard_map/ppermute | solution.py:21
  415.2 6.2 collective-permute-start.7
  421.5 39.5 %collective-permute-done.7 = bf16[2048,128]{1,0:T(8,128)(2,1)S(1)} collective-permute-done((bf16[2048,128]{1,0:T(8,128)(2,1)S(1)}, bf16[2048,128]{1,0:T(8,128)(2,1)S(1)}, u32[]{:S(2)}, u32[]{:S(2)}) %collective-permute-start.7) | collective-permute-done | bytes 524320 | tf_op jit(solution)/shard_map/ppermute | solution.py:21
  465.6 40.2 %collective-permute-done.8 = bf16[2048,128]{1,0:T(8,128)(2,1)} collective-permute-done((bf16[2048,128]{1,0:T(8,128)(2,1)S(1)}, bf16[2048,128]{1,0:T(8,128)(2,1)}, u32[]{:S(2)}, u32[]{:S(2)}) %collective-permute-start.8) | collective-permute-done | bytes 524320 | tf_op jit(solution)/shard_map/ppermute | solution.py:21
  512.5 18.8 %collective-permute-done.9 = bf16[2048,128]{1,0:T(8,128)(2,1)S(1)} collective-permute-done((bf16[2048,128]{1,0:T(8,128)(2,1)S(1)}, bf16[2048,128]{1,0:T(8,128)(2,1)S(1)}, u32[]{:S(2)}, u32[]{:S(2)}) %collective-permute-start.9) | collective-permute-done | bytes 524320 | tf_op jit(solution)/shard_map/ppermute | solution.py:21
  537.5 185.4 %reduce-scatter.5.cloned.1.call-done = f32[16,64]{1,0:T(8,128)} async-done(((f32[2048,64]{1,0:T(8,128)}), f32[16,64]{1,0:T(8,128)}) %reduce-scatter.5.cloned.1.call-update) | async-done | bytes 4112 | tf_op jit(solution)/shard_map/reduce_scatter | solution.py:29
  724.5 2.1 reshape.26
  726.6 13.6 %all-to-all-start.1 = ((bf16[128,2,512]{2,1,0:T(2,128)(2,1)}), bf16[128,2,512]{2,1,0:T(2,128)(2,1)S(1)}, u32[]{:S(2)}, u32[]{:S(2)}) async-start(bf16[128,2,512]{2,1,0:T(2,128)(2,1)} %reshape.26), calls=%async_computation.3 | async-start | bytes 524288 | tf_op jit(solution)/shard_map/all_to_all | solution.py:10
  745.6 4.1 collective-permute-start.11
  751.7 9.8 %all-to-all-done.1 = bf16[128,2,512]{2,1,0:T(2,128)(2,1)S(1)} async-done(((bf16[128,2,512]{2,1,0:T(2,128)(2,1)}), bf16[128,2,512]{2,1,0:T(2,128)(2,1)S(1)}, u32[]{:S(2)}, u32[]{:S(2)}) %all-to-all-start.1) | async-done | bytes 262176 | tf_op jit(solution)/shard_map/all_to_all | solution.py:10
  767.1 2.8 collective-permute-start.12
  773.9 8.6 collective-permute-done.12
  788.8 56.0 %all-reduce.3.cloned.1.call-done = (bf16[1,128,128]{1,2,0:T(8,128)(2,1)}, bf16[1,128,128]{1,2,0:T(8,128)(2,1)}, bf16[1,128,128]{1,2,0:T(8,128)(2,1)}, bf16[1,128...) async-done(((bf16[1,128,128]{1,2,0:T(8,128)(2,1)}, ...) | async-done | bytes 491536 | tf_op jit(solution)/shard_map/psum | solution.py:78
  (182 shorter events, 80.2 us)
Async XLA Ops:
  7.2 406.0 %copy-start = (bf16[64,128]{1,0:T(8,128)(2,1)S(1)}, bf16[64,128]{1,0:T(8,128)(2,1)}, u32[]{:S(2)}) copy-start(bf16[64,128]{1,0:T(8,128)(2,1)} %param.10) | copy-start | bytes 49156
  7.2 322.9 %reduce-scatter.3.cloned.1.call-start = ((), (), s32[]{:S(2)}) async-start(), calls=%async_computation.4 | async-start | bytes 1056768 | tf_op jit(solution)/shard_map/reduce_scatter | solution.py:29
  7.2 4.1 collective-permute-start
  12.2 19.9 %collective-permute-start.1 = (bf16[2048,128]{1,0:T(8,128)(2,1)S(1)}, bf16[2048,128]{1,0:T(8,128)(2,1)S(1)}, u32[]{:S(2)}, u32[]{:S(2)}) collective-permute-start(bf16[2048,128]{1,0:T(8,128)(2,1)S(1)} %fusion.1), channel_id=1, source_target_pairs={{0,2},{2,0},{1,3},{3,1},{4,6},{6,4},{5,7},{7,5},{8,10},{10,8},{9,1... | collective-permute-start | bytes 1572872 | tf_op jit(solution)/shard_map/ppermute | solution.py:21
  32.9 16.8 %collective-permute-start.2 = (bf16[2048,128]{1,0:T(8,128)(2,1)S(1)}, bf16[2048,128]{1,0:T(8,128)(2,1)S(1)}, u32[]{:S(2)}, u32[]{:S(2)}) collective-permute-start(bf16[2048,128]{1,0:T(8,128)(2,1)S(1)} %fusion.2), channel_id=1, source_target_pairs={{0,4},{4,0},{1,5},{5,1},{2,6},{6,2},{3,7},{7,3},{8,12},{12,8},{9,1... | collective-permute-start | bytes 1572872 | tf_op jit(solution)/shard_map/ppermute | solution.py:21
  50.6 14.4 %collective-permute-start.3 = (bf16[2048,128]{1,0:T(8,128)(2,1)S(1)}, bf16[2048,128]{1,0:T(8,128)(2,1)S(1)}, u32[]{:S(2)}, u32[]{:S(2)}) collective-permute-start(bf16[2048,128]{1,0:T(8,128)(2,1)S(1)} %fusion.3), channel_id=1, source_target_pairs={{0,8},{8,0},{1,9},{9,1},{2,10},{10,2},{3,11},{11,3},{4,12},{12,4},... | collective-permute-start | bytes 1572872 | tf_op jit(solution)/shard_map/ppermute | solution.py:21
  65.8 25.6 %collective-permute-start.4 = (bf16[2048,128]{1,0:T(8,128)(2,1)S(1)}, bf16[2048,128]{1,0:T(8,128)(2,1)S(1)}, u32[]{:S(2)}, u32[]{:S(2)}) collective-permute-start(bf16[2048,128]{1,0:T(8,128)(2,1)S(1)} %fusion.4), channel_id=1, source_target_pairs={{0,16},{16,0},{1,17},{17,1},{2,18},{18,2},{3,19},{19,3},{4,20},{20... | collective-permute-start | bytes 1572872 | tf_op jit(solution)/shard_map/ppermute | solution.py:21
  92.3 253.1 %copy-start.6 = (bf16[2048,128]{1,0:T(8,128)(2,1)}, bf16[2048,128]{1,0:T(8,128)(2,1)S(1)}, u32[]{:S(2)}) copy-start(bf16[2048,128]{1,0:T(8,128)(2,1)S(1)} %fusion.5) | copy-start | bytes 1572868
  92.3 254.1 %collective-permute-start.5 = (bf16[2048,128]{1,0:T(8,128)(2,1)S(1)}, bf16[2048,128]{1,0:T(8,128)(2,1)S(1)}, u32[]{:S(2)}, u32[]{:S(2)}) collective-permute-start(bf16[2048,128]{1,0:T(8,128)(2,1)S(1)} %fusion.5), channel_id=1, source_target_pairs={{0,32},{32,0},{1,33},{33,1},{2,34},{34,2},{3,35},{35,3},{4,36},{36... | collective-permute-start | bytes 1572872 | tf_op jit(solution)/shard_map/ppermute | solution.py:21
  331.8 34.7 %all-to-all-start = ((bf16[128,2,512]{2,1,0:T(2,128)(2,1)}), bf16[128,2,512]{2,1,0:T(2,128)(2,1)S(1)}, u32[]{:S(2)}, u32[]{:S(2)}) async-start(bf16[128,2,512]{2,1,0:T(2,128)(2,1)} %reshape.24), calls=%async_computation.1 | async-start | bytes 524288 | tf_op jit(solution)/shard_map/all_to_all | solution.py:10
  345.3 377.7 %reduce-scatter.5.cloned.1.call-start = ((), (), s32[]{:S(2)}) async-start(), calls=%async_computation.5 | async-start | bytes 1056768 | tf_op jit(solution)/shard_map/reduce_scatter | solution.py:29
  347.5 64.8 %collective-permute-start.6 = (bf16[2048,128]{1,0:T(8,128)(2,1)S(1)}, bf16[2048,128]{1,0:T(8,128)(2,1)S(1)}, u32[]{:S(2)}, u32[]{:S(2)}) collective-permute-start(bf16[2048,128]{1,0:T(8,128)(2,1)S(1)} %fusion.6), channel_id=1, source_target_pairs={{0,64},{64,0},{1,65},{65,1},{2,66},{66,2},{3,67},{67,3},{4,68},{68... | collective-permute-start | bytes 1572872 | tf_op jit(solution)/shard_map/ppermute | solution.py:21
  367.7 44.6 %copy-start.27 = (bf16[7,128,128]{2,1,0:T(8,128)(2,1)S(1)}, bf16[7,128,128]{2,1,0:T(8,128)(2,1)}, u32[]{:S(2)}) copy-start(bf16[7,128,128]{2,1,0:T(8,128)(2,1)} %param.8) | copy-start | bytes 688132
  368.8 44.3 %copy-start.10 = (bf16[128,16,64]{2,1,0:T(8,128)(2,1)S(1)}, bf16[128,16,64]{2,1,0:T(8,128)(2,1)}, u32[]{:S(2)}) copy-start(bf16[128,16,64]{2,1,0:T(8,128)(2,1)} %reshape.25) | copy-start | bytes 786436
  368.8 44.3 %copy-start.45 = (bf16[2048,128]{1,0:T(8,128)(2,1)S(1)}, bf16[2048,128]{1,0:T(8,128)(2,1)}, u32[]{:S(2)}) copy-start(bf16[2048,128]{1,0:T(8,128)(2,1)} %param.11) | copy-start | bytes 1572868
  415.2 45.8 %collective-permute-start.7 = (bf16[2048,128]{1,0:T(8,128)(2,1)S(1)}, bf16[2048,128]{1,0:T(8,128)(2,1)S(1)}, u32[]{:S(2)}, u32[]{:S(2)}) collective-permute-start(bf16[2048,128]{1,0:T(8,128)(2,1)S(1)} %convolution_convert_fusion.6), channel_id=1, source_target_pairs={{0,64},{64,0},{1,65},{65,1},{2,66},{66,2},{3,67},{67,3},{4,68},{68... | collective-permute-start | bytes 1572872 | tf_op jit(solution)/shard_map/ppermute | solution.py:21
  462.4 43.4 %collective-permute-start.8 = (bf16[2048,128]{1,0:T(8,128)(2,1)S(1)}, bf16[2048,128]{1,0:T(8,128)(2,1)}, u32[]{:S(2)}, u32[]{:S(2)}) collective-permute-start(bf16[2048,128]{1,0:T(8,128)(2,1)S(1)} %convolution_convert_fusion.5), channel_id=1, source_target_pairs={{0,32},{32,0},{1,33},{33,1},{2,34},{34,2},{3,35},{35,3},{4,36},{36... | collective-permute-start | bytes 1572872 | tf_op jit(solution)/shard_map/ppermute | solution.py:21
  507.5 23.8 %collective-permute-start.9 = (bf16[2048,128]{1,0:T(8,128)(2,1)S(1)}, bf16[2048,128]{1,0:T(8,128)(2,1)S(1)}, u32[]{:S(2)}, u32[]{:S(2)}) collective-permute-start(bf16[2048,128]{1,0:T(8,128)(2,1)S(1)} %convolution_convert_fusion.4), channel_id=1, source_target_pairs={{0,16},{16,0},{1,17},{17,1},{2,18},{18,2},{3,19},{19,3},{4,20},{20... | collective-permute-start | bytes 1572872 | tf_op jit(solution)/shard_map/ppermute | solution.py:21
  533.5 208.9 %collective-permute-start.10 = (bf16[2048,128]{1,0:T(8,128)(2,1)}, bf16[2048,128]{1,0:T(8,128)(2,1)}, u32[]{:S(2)}, u32[]{:S(2)}) collective-permute-start(bf16[2048,128]{1,0:T(8,128)(2,1)} %convolution_convert_fusion.3), channel_id=1, source_target_pairs={{0,8},{8,0},{1,9},{9,1},{2,10},{10,2},{3,11},{11,3},{4,12},{12,4},... | collective-permute-start | bytes 1572872 | tf_op jit(solution)/shard_map/ppermute | solution.py:21
  726.6 34.9 %all-to-all-start.1 = ((bf16[128,2,512]{2,1,0:T(2,128)(2,1)}), bf16[128,2,512]{2,1,0:T(2,128)(2,1)S(1)}, u32[]{:S(2)}, u32[]{:S(2)}) async-start(bf16[128,2,512]{2,1,0:T(2,128)(2,1)} %reshape.26), calls=%async_computation.3 | async-start | bytes 524288 | tf_op jit(solution)/shard_map/all_to_all | solution.py:10
  740.3 104.5 %all-reduce.3.cloned.1.call-start = ((), (), s32[]{:S(2)}) async-start(), calls=%async_computation.6 | async-start | bytes 983040 | tf_op jit(solution)/shard_map/psum | solution.py:78
  745.6 19.0 %collective-permute-start.11 = (bf16[2048,128]{1,0:T(8,128)(2,1)}, bf16[2048,128]{1,0:T(8,128)(2,1)}, u32[]{:S(2)}, u32[]{:S(2)}) collective-permute-start(bf16[2048,128]{1,0:T(8,128)(2,1)} %convolution_convert_fusion.2), channel_id=1, source_target_pairs={{0,4},{4,0},{1,5},{5,1},{2,6},{6,2},{3,7},{7,3},{8,12},{12,8},{9,1... | collective-permute-start | bytes 1572872 | tf_op jit(solution)/shard_map/ppermute | solution.py:21
  767.1 15.4 %collective-permute-start.12 = (bf16[2048,128]{1,0:T(8,128)(2,1)S(1)}, bf16[2048,128]{1,0:T(8,128)(2,1)S(1)}, u32[]{:S(2)}, u32[]{:S(2)}) collective-permute-start(bf16[2048,128]{1,0:T(8,128)(2,1)S(1)} %convolution_convert_fusion.1), channel_id=1, source_target_pairs={{0,2},{2,0},{1,3},{3,1},{4,6},{6,4},{5,7},{7,5},{8,10},{10,8},{9,1... | collective-permute-start | bytes 1572872 | tf_op jit(solution)/shard_map/ppermute | solution.py:21
  786.9 71.0 %collective-permute-start.13 = (bf16[2048,128]{1,0:T(8,128)(2,1)S(1)}, bf16[2048,128]{1,0:T(8,128)(2,1)S(1)}, u32[]{:S(2)}, u32[]{:S(2)}) collective-permute-start(bf16[2048,128]{1,0:T(8,128)(2,1)S(1)} %convolution_convert_fusion), channel_id=1, source_target_pairs={{0,1},{1,0},{2,3},{3,2},{4,5},{5,4},{6,7},{7,6},{8,9},{9,8},{10,11... | collective-permute-start | bytes 1572872 | tf_op jit(solution)/shard_map/ppermute | solution.py:21
  (41 other events, 134.6 us)
Sparse Core Ops, SparseCore 0:
  69.2 260.8 reduce-scatter.2
  465.7 257.1 reduce-scatter.4
  785.7 59.1 all-reduce.2
